TPU v7x, 128 devices: a whole 4x4x4 slice. The times are simulated.
128 devices in a mesh: replica: 2 (over z_lo), shard: 64 (over x, y, z_hi, core).
Axes of the slice: x: 4, y: 4, z: 4 (z_hi: 2, z_lo: 2; z = z_hi * 2 + z_lo), core: 2. Of those that a mesh axis runs over, the one named last changes fastest.
Arguments:
- tokens: bfloat16 [131072, 960], P(('replica', 'shard')), may hold values from -6 to 6
- cotangent: bfloat16 [131072, 960], P(('replica', 'shard')), may hold values from -6 to 6
- query_weight: bfloat16 [960, 960], P('shard'), may hold values from -1 to 1
- key_weight: bfloat16 [960, 320], P('shard'), may hold values from -1 to 1
- value_weight: bfloat16 [960, 320], P('shard'), may hold values from -0.1875 to 0.1875
- w_gate: bfloat16 [960, 2560], P('shard'), may hold values from -0.1875 to 0.1875
- w_up: bfloat16 [960, 2560], P('shard'), may hold values from -0.1875 to 0.1875
- output_weight: bfloat16 [960, 960], P(None, 'shard'), may hold values from -0.75 to 0.75
- w_down: bfloat16 [2560, 960], P(None, 'shard'), may hold values from -0.125 to 0.125
- norm_attn: bfloat16 [960], P('shard'), may hold values from 0.5 to 1.5
- norm_ffn: bfloat16 [960], P('shard'), may hold values from 0.5 to 1.5
Outputs:
- output: bfloat16 [131072, 960], P(('replica', 'shard'))
- grad_tokens: float32 [131072, 960], P(('replica', 'shard'))
- grad_query: float32 [960, 960], P('shard')
- grad_key: float32 [960, 320], P('shard')
- grad_value: float32 [960, 320], P('shard')
- grad_gate: float32 [960, 2560], P('shard')
- grad_up: float32 [960, 2560], P('shard')
- grad_out: float32 [960, 960], P(None, 'shard')
- grad_down: float32 [2560, 960], P(None, 'shard')
- grad_norm_attn: float32 [960], P('shard')
- grad_norm_ffn: float32 [960], P('shard')
All inputs are finite; a program needn't handle non-finite values.
Results may differ from a plain program's by a relative error of at most 0.018.
The roundings to bfloat16 on the way count: a program that leaves them out, or rounds other values in their place, can miss the bound.
Values may be sent and summed in bfloat16 or wider, within the bound.
A program may use at most 256 MiB of HBM per device.

v0:
```python
import math
import jax
import jax.numpy as jnp
from jax import lax
from jax.sharding import PartitionSpec as P

HQ = 15
KEY_VALUE_HEADS = 5
HEAD_SIZE = 64
SEQUENCE_TOKENS = 512
QUERY_PER_KEY = 3
EPSILON = 1e-05


def gather_turned(arrays, axis, dims):
    turned = [jnp.moveaxis(a, dim, 0) for a, dim in zip(arrays, dims)]
    both = jnp.concatenate([t.reshape(len(t), -1) for t in turned], axis=1)
    whole, at, finished = (lax.all_gather(both, axis, axis=0, tiled=True), 0, [])
    for t, dim in zip(turned, dims):
        section = whole[:, at : at + t[0].size].reshape(-1, *t.shape[1:])
        finished.append(jnp.moveaxis(section, 0, dim))
        at += t[0].size
    return tuple(finished)


def packed_total(arrays, axis):
    vector, at, finished = (jnp.concatenate([a.reshape(-1) for a in arrays]), 0, [])
    so_far = lax.psum(vector, axis)
    for a in arrays:
        finished.append(so_far[at : at + a.size].reshape(a.shape))
        at += a.size
    return tuple(finished)


def swap_half_pairs(values):
    middle = values.shape[-1] // 2
    return jnp.concatenate([-values[..., middle:], values[..., :middle]], axis=-1)


def rope_tables():
    half_dim = HEAD_SIZE // 2
    rates = jnp.exp(
        jnp.arange(half_dim, dtype=jnp.float32) * (-2.0 * math.log(10000.0) / HEAD_SIZE)
    )
    angles = jnp.arange(SEQUENCE_TOKENS, dtype=jnp.float32)[:, None] * rates[None, :]
    angles = jnp.concatenate([angles, angles], axis=-1)
    return (jnp.cos(angles), jnp.sin(angles))


def causal_mask():
    row_ids = lax.broadcasted_iota(jnp.int32, (SEQUENCE_TOKENS, SEQUENCE_TOKENS), 0)
    col_ids = lax.broadcasted_iota(jnp.int32, (SEQUENCE_TOKENS, SEQUENCE_TOKENS), 1)
    return col_ids <= row_ids


def score_block(queries, key_block):
    scores = jnp.einsum(
        "qkgd,tkd->kgqt", queries, key_block, preferred_element_type=jnp.float32
    ) * (1.0 / math.sqrt(HEAD_SIZE))
    return jnp.where(causal_mask(), scores, -1e30)


def attend_forward(packed_in):
    queries, key_block, values = packed_in
    scores = score_block(queries, key_block)
    row_top = jnp.max(scores, axis=-1)
    log_total = row_top + jnp.log(jnp.sum(jnp.exp(scores - row_top[..., None]), axis=-1))
    soft_low = jnp.exp(scores - log_total[..., None]).astype(jnp.bfloat16)
    heads_out = jnp.einsum(
        "kgqt,tkd->qkgd", soft_low, values, preferred_element_type=jnp.float32
    ).astype(jnp.bfloat16)
    return (heads_out, log_total)


def attend_backward(packed_in):
    queries, key_block, values, heads_out, log_total, head_output_gradient = packed_in
    scores = score_block(queries, key_block)
    soft_full = jnp.exp(scores - log_total[..., None])
    soft_low = soft_full.astype(jnp.bfloat16)
    value_rows_gradient = jnp.einsum(
        "kgqt,qkgd->tkd", soft_low, head_output_gradient, preferred_element_type=jnp.float32
    )
    grad_soft = jnp.einsum(
        "qkgd,tkd->kgqt", head_output_gradient, values, preferred_element_type=jnp.float32
    )
    offset = jnp.transpose(
        jnp.sum(head_output_gradient.astype(jnp.float32) * heads_out.astype(jnp.float32), axis=-1),
        (1, 2, 0),
    )
    grad_scores = (soft_full * (grad_soft - offset[..., None])).astype(jnp.bfloat16)
    scale = 1.0 / math.sqrt(HEAD_SIZE)
    grad_queries = (
        jnp.einsum("kgqt,tkd->qkgd", grad_scores, key_block, preferred_element_type=jnp.float32)
        * scale
    )
    key_rows_gradient = (
        jnp.einsum("kgqt,qkgd->tkd", grad_scores, queries, preferred_element_type=jnp.float32)
        * scale
    )
    return (grad_queries, key_rows_gradient, value_rows_gradient)


def tdot(left, right):
    return lax.dot_general(
        left, right, (((0,), (0,)), ((), ())), preferred_element_type=jnp.float32
    )


def contract_product(left, weight):
    return lax.dot_general(
        left, weight, (((1,), (1,)), ((), ())), preferred_element_type=jnp.float32
    )


def forward(tokens, weights):
    (
        query_weight,
        key_weight,
        value_weight,
        w_gate,
        w_up,
        output_weight,
        w_down,
        norm_attn,
        norm_ffn,
    ) = weights
    count_of_rows = tokens.shape[0]
    sequence_count = count_of_rows // SEQUENCE_TOKENS
    inputs = tokens.astype(jnp.float32)
    recip_attn = lax.rsqrt(jnp.mean(inputs * inputs, axis=-1, keepdims=True) + EPSILON)
    attention_normalized = (inputs * recip_attn * norm_attn.astype(jnp.float32)).astype(
        jnp.bfloat16
    )
    cosine_table, sine_table = rope_tables()
    rotated_query = jnp.dot(
        attention_normalized, query_weight, preferred_element_type=jnp.float32
    ).reshape(sequence_count, SEQUENCE_TOKENS, KEY_VALUE_HEADS, QUERY_PER_KEY, HEAD_SIZE)
    rotated_query = (
        rotated_query * cosine_table[:, None, None, :]
        + swap_half_pairs(rotated_query) * sine_table[:, None, None, :]
    ).astype(jnp.bfloat16)
    rotated_key = jnp.dot(
        attention_normalized, key_weight, preferred_element_type=jnp.float32
    ).reshape(sequence_count, SEQUENCE_TOKENS, KEY_VALUE_HEADS, HEAD_SIZE)
    rotated_key = (
        rotated_key * cosine_table[:, None, :]
        + swap_half_pairs(rotated_key) * sine_table[:, None, :]
    ).astype(jnp.bfloat16)
    value_per_head = (
        jnp.dot(attention_normalized, value_weight, preferred_element_type=jnp.float32)
        .astype(jnp.bfloat16)
        .reshape(sequence_count, SEQUENCE_TOKENS, KEY_VALUE_HEADS, HEAD_SIZE)
    )
    heads_out, log_total = lax.map(attend_forward, (rotated_query, rotated_key, value_per_head))
    attended = heads_out.reshape(count_of_rows, HQ * HEAD_SIZE)
    hidden = inputs + jnp.dot(attended, output_weight, preferred_element_type=jnp.float32)
    recip_ffn = lax.rsqrt(jnp.mean(hidden * hidden, axis=-1, keepdims=True) + EPSILON)
    normed_ffn = (hidden * recip_ffn * norm_ffn.astype(jnp.float32)).astype(jnp.bfloat16)
    gate_pre = jnp.dot(normed_ffn, w_gate, preferred_element_type=jnp.float32)
    upward = jnp.dot(normed_ffn, w_up, preferred_element_type=jnp.float32)
    sigmoid_gate = jax.nn.sigmoid(gate_pre)
    activated = (gate_pre * sigmoid_gate * upward).astype(jnp.bfloat16)
    output = (hidden + jnp.dot(activated, w_down, preferred_element_type=jnp.float32)).astype(
        jnp.bfloat16
    )
    saved = (
        inputs,
        recip_attn,
        attention_normalized,
        rotated_query,
        rotated_key,
        value_per_head,
        heads_out,
        log_total,
        hidden,
        recip_ffn,
        normed_ffn,
        gate_pre,
        upward,
        sigmoid_gate,
        activated,
    )
    return (output, saved)


def ffn_backward(saved, cotangent, weights):
    (
        query_weight,
        key_weight,
        value_weight,
        w_gate,
        w_up,
        output_weight,
        w_down,
        norm_attn,
        norm_ffn,
    ) = weights
    (
        inputs,
        recip_attn,
        attention_normalized,
        rotated_query,
        rotated_key,
        value_per_head,
        heads_out,
        log_total,
        hidden,
        recip_ffn,
        normed_ffn,
        gate_pre,
        upward,
        sigmoid_gate,
        activated,
    ) = saved
    grad_w_down = tdot(activated, cotangent)
    grad_act = contract_product(cotangent, w_down)
    gate_slope = sigmoid_gate * (1.0 + gate_pre * (1.0 - sigmoid_gate))
    grad_gate_low = (grad_act * upward * gate_slope).astype(jnp.bfloat16)
    grad_upward_low = (grad_act * gate_pre * sigmoid_gate).astype(jnp.bfloat16)
    grad_w_gate = tdot(normed_ffn, grad_gate_low)
    grad_w_up = tdot(normed_ffn, grad_upward_low)
    grad_normed = contract_product(grad_gate_low, w_gate) + contract_product(grad_upward_low, w_up)
    grad_norm_ffn = jnp.sum(grad_normed * hidden * recip_ffn, axis=0)
    scaled = grad_normed * norm_ffn.astype(jnp.float32)
    grad_hidden = (
        cotangent.astype(jnp.float32)
        + recip_ffn * scaled
        - hidden * recip_ffn**3 * jnp.mean(scaled * hidden, axis=-1, keepdims=True)
    )
    return (grad_hidden, (grad_w_gate, grad_w_up, grad_w_down, grad_norm_ffn))


def attn_backward(saved, grad_hidden, weights):
    (
        query_weight,
        key_weight,
        value_weight,
        w_gate,
        w_up,
        output_weight,
        w_down,
        norm_attn,
        norm_ffn,
    ) = weights
    (
        inputs,
        recip_attn,
        attention_normalized,
        rotated_query,
        rotated_key,
        value_per_head,
        heads_out,
        log_total,
        hidden,
        recip_ffn,
        normed_ffn,
        gate_pre,
        upward,
        sigmoid_gate,
        activated,
    ) = saved
    count_of_rows = inputs.shape[0]
    sequence_count = count_of_rows // SEQUENCE_TOKENS
    cosine_table, sine_table = rope_tables()
    hidden_gradient_narrow = grad_hidden.astype(jnp.bfloat16)
    attended = heads_out.reshape(count_of_rows, HQ * HEAD_SIZE)
    grad_w_out = tdot(attended, hidden_gradient_narrow)
    head_output_gradient = (
        contract_product(hidden_gradient_narrow, output_weight)
        .astype(jnp.bfloat16)
        .reshape(sequence_count, SEQUENCE_TOKENS, KEY_VALUE_HEADS, QUERY_PER_KEY, HEAD_SIZE)
    )
    grad_queries, key_rows_gradient, value_rows_gradient = lax.map(
        attend_backward,
        (rotated_query, rotated_key, value_per_head, heads_out, log_total, head_output_gradient),
    )
    grad_queries = (
        (
            grad_queries * cosine_table[:, None, None, :]
            - swap_half_pairs(grad_queries) * sine_table[:, None, None, :]
        )
        .astype(jnp.bfloat16)
        .reshape(count_of_rows, HQ * HEAD_SIZE)
    )
    key_rows_gradient = (
        (
            key_rows_gradient * cosine_table[:, None, :]
            - swap_half_pairs(key_rows_gradient) * sine_table[:, None, :]
        )
        .astype(jnp.bfloat16)
        .reshape(count_of_rows, KEY_VALUE_HEADS * HEAD_SIZE)
    )
    value_rows_gradient = value_rows_gradient.astype(jnp.bfloat16).reshape(
        count_of_rows, KEY_VALUE_HEADS * HEAD_SIZE
    )
    grad_w_query = tdot(attention_normalized, grad_queries)
    grad_w_key = tdot(attention_normalized, key_rows_gradient)
    grad_w_value = tdot(attention_normalized, value_rows_gradient)
    grad_normed_attn = (
        contract_product(grad_queries, query_weight)
        + contract_product(key_rows_gradient, key_weight)
        + contract_product(value_rows_gradient, value_weight)
    )
    grad_norm_attn = jnp.sum(grad_normed_attn * inputs * recip_attn, axis=0)
    scaled_attn = grad_normed_attn * norm_attn.astype(jnp.float32)
    grad_tokens = (
        grad_hidden
        + recip_attn * scaled_attn
        - inputs * recip_attn**3 * jnp.mean(scaled_attn * inputs, axis=-1, keepdims=True)
    )
    return (grad_tokens, (grad_w_query, grad_w_key, grad_w_value, grad_w_out, grad_norm_attn))


def shards(
    tokens,
    cotangent,
    query_weight,
    key_weight,
    value_weight,
    w_gate,
    w_up,
    output_weight,
    w_down,
    norm_attn,
    norm_ffn,
):
    gathered = gather_turned(
        (
            query_weight,
            key_weight,
            value_weight,
            w_gate,
            w_up,
            output_weight,
            w_down,
            norm_attn,
            norm_ffn,
        ),
        "shard",
        (0, 0, 0, 0, 0, 1, 1, 0, 0),
    )
    output, saved = forward(tokens, gathered)
    back_weights = gather_turned(
        (
            query_weight,
            key_weight,
            value_weight,
            w_gate,
            w_up,
            output_weight,
            w_down,
            norm_attn,
            norm_ffn,
        ),
        "shard",
        (0, 0, 0, 0, 0, 1, 1, 0, 0),
    )
    grad_hidden, ffn_grads = ffn_backward(saved, cotangent, back_weights)
    g_gate, g_up, g_down, g_norm_ffn = ffn_grads
    grad_tokens, attn_grads = attn_backward(saved, grad_hidden, back_weights)
    g_query, g_key, g_value, g_out, g_norm_attn = attn_grads
    owned = (
        lax.psum_scatter(g_query, "shard", scatter_dimension=0, tiled=True),
        lax.psum_scatter(g_key, "shard", scatter_dimension=0, tiled=True),
        lax.psum_scatter(g_value, "shard", scatter_dimension=0, tiled=True),
        lax.psum_scatter(g_gate, "shard", scatter_dimension=0, tiled=True),
        lax.psum_scatter(g_up, "shard", scatter_dimension=0, tiled=True),
        lax.psum_scatter(g_out, "shard", scatter_dimension=1, tiled=True),
        lax.psum_scatter(g_down, "shard", scatter_dimension=1, tiled=True),
        lax.psum_scatter(g_norm_attn, "shard", scatter_dimension=0, tiled=True),
        lax.psum_scatter(g_norm_ffn, "shard", scatter_dimension=0, tiled=True),
    )
    o_query, o_key, o_value, o_gate, o_up, o_out, o_down, o_norm_attn, o_norm_ffn = owned
    shares = tuple(
        (
            part.astype(jnp.float32)
            for part in packed_total(
                (
                    o_query.astype(jnp.bfloat16),
                    o_key.astype(jnp.bfloat16),
                    o_value.astype(jnp.bfloat16),
                    o_gate.astype(jnp.bfloat16),
                    o_up.astype(jnp.bfloat16),
                    o_out.astype(jnp.bfloat16),
                    o_down.astype(jnp.bfloat16),
                    o_norm_attn.astype(jnp.bfloat16),
                    o_norm_ffn.astype(jnp.bfloat16),
                ),
                "replica",
            )
        )
    )
    s_query, s_key, s_value, s_gate, s_up, s_out, s_down, s_norm_attn, s_norm_ffn = shares
    return (
        output,
        grad_tokens,
        s_query,
        s_key,
        s_value,
        s_gate,
        s_up,
        s_out,
        s_down,
        s_norm_attn,
        s_norm_ffn,
    )


def solution(mesh):
    in_specs = (
        P(("replica", "shard"), None),
        P(("replica", "shard"), None),
        P("shard", None),
        P("shard", None),
        P("shard", None),
        P("shard", None),
        P("shard", None),
        P(None, "shard"),
        P(None, "shard"),
        P("shard"),
        P("shard"),
    )
    out_specs = (
        P(("replica", "shard"), None),
        P(("replica", "shard"), None),
        P("shard", None),
        P("shard", None),
        P("shard", None),
        P("shard", None),
        P("shard", None),
        P(None, "shard"),
        P(None, "shard"),
        P("shard"),
        P("shard"),
    )
    return jax.shard_map(shards, mesh=mesh, in_specs=in_specs, out_specs=out_specs, check_vma=False)
```

profile of v0, /device:TPU:1, one launch (start us, length us, event | category | flops | bytes accessed | tf_op | source)
XLA Modules:
  0.0 1250.7 jit_solution(898325108105369608)
XLA Ops:
  16.5 118.3 %all-gather.3.cloned.1.call-done = bf16[64,15,10242]{2,1,0:T(8,128)(2,1)} async-done(((bf16[1,15,10242]{2,1,0:T(8,128)(2,1)}), bf16[64,15,10242]{2,1,0:T(8,128)(2,1)}) %all-gather.3.cloned.1.call-update) | async-done | bytes 19664656 | tf_op jit(solution)/shard_map/all_gather | solution.py:18
  134.8 20.1 %reshape.306 = bf16[960,10242]{1,0:T(8,128)(2,1)} reshape(bf16[64,15,10242]{2,1,0:T(8,128)(2,1)} %all-gather.3.cloned.1.call-done) | data formatting | bytes 39329280
  172.2 6.4 reshape.282
  184.9 50.4 %while.26 = (s32[]{:T(128)}, bf16[2,512,5,3,64]{1,4,3,2,0:T(8,128)(2,1)}, f32[2,5,3,512]{3,2,1,0:T(4,128)}, bf16[2,512,5,64]{1,3,2,0:T(8,128)(2,1)S(1)}, bf16[2,...) while((s32[]{:T(128)}, bf16[2,512,5,3,64]{1,4,3,2,0:T(8,128)(2,1)}, ...), condition=%wide.region_4.5_spmd, body=%wide.region_1.4_spmd.sunk | while | flops 1050632704 | bytes 67375304 | solution.py:154
  185.0 6.9 fusion.180
  191.9 8.9 exponential_reduce_fusion.2
  200.9 7.8 fusion.181
  210.0 6.9 fusion.180
  217.0 8.9 exponential_reduce_fusion.2
  225.9 7.8 fusion.181
  246.6 11.7 fusion.78
  258.3 10.7 fusion.68
  269.0 19.1 %fusion.65 = (bf16[1024,2560]{1,0:T(8,128)(2,1)}, bf16[1024,2560]{1,0:T(8,128)(2,1)}, bf16[1024,2560]{1,0:T(8,128)(2,1)}) fusion(f32[2560,1024]{0,1:T(8,128)} %fusion.68, f32[1024,2560]{1,0:T(8,128)} %fusion.78, bf16[1024,960]{0,1:T(8,128)(2,1)} %copy-done.23, bf16[960,10242]{1,0:T(8,128)(2,1)} %reshape.306), kind=kOutput, calls=%fused_computation.68 | convolution fusion | flops 5075107840 | bytes 43581440 | tf_op jit(solution)/shard_map/dot_general | solution.py:160
  288.1 9.1 fusion.72
  297.3 9.1 multiply_reduce_fusion
  318.0 6.2 reshape.284
  327.4 59.5 %while.27 = (s32[]{:T(128)}, f32[2,512,5,3,64]{1,4,3,2,0:T(8,128)}, f32[2,512,5,64]{1,3,2,0:T(8,128)}, bf16[2,512,5,64]{1,3,2,0:T(8,128)(2,1)}, bf16[2,512,5,64]...) while((s32[]{:T(128)}, f32[2,512,5,3,64]{1,4,3,2,0:T(8,128)}, ...), condition=%wide.region_9.10_spmd, body=%wide.region_7.9_spmd.sunk | while | flops 2558779904 | bytes 186770704 | solution.py:273
  342.6 8.6 fusion.194
  372.3 8.6 fusion.194
  412.7 8.0 fusion.136
  420.7 7.7 fusion.137
  428.5 9.0 add_convert_fusion
  437.4 7.8 fusion.138
  448.3 463.7 %fusion.127 = (f32[16,960]{1,0:T(8,128)S(1)}, f32[16,320]{1,0:T(8,128)S(1)}, f32[16,320]{1,0:T(8,128)S(1)}, f32[16,2560]{1,0:T(8,128)S(1)}, f32[16,2560]{1,0:T(8...) fusion(f32[960,960]{1,0:T(8,128)} %fusion.122, f32[960,320]{1,0:T(8,128)} %fusion.120, ...), kind=kCustom, calls=%all-reduce-scatter.7 | all-reduce-scatter fusion | flops 10485761 | bytes 39977472
  913.4 8.0 collective-permute-start.10
  926.5 7.2 fusion.87
  937.0 164.9 %all-reduce.16 = (bf16[960]{0:T(1024)(128)(2,1)S(1)}, bf16[960]{0:T(1024)(128)(2,1)S(1)}) all-reduce(f32[960]{0:T(1024)S(1)} %get-tuple-element.177, f32[960]{0:T(1024)S(1)} %copy-done.38), channel_id=9, replica_groups=mesh['replica'=2,'shard'=64] {'shard'}, use_global_device_ids=true, to_apply=%region_19.20.clone | all-reduce | flops 1920 | bytes 11520
  1158.5 6.7 collective-permute-start.19
  1175.7 9.9 collective-permute-start.15
  1190.7 8.3 concatenate.45
  1199.0 6.2 fusion.84
  1205.2 27.0 %all-reduce.20.cloned.1.call-done = bf16[153630]{0:T(1024)(128)(2,1)} async-done(((bf16[153630]{0:T(1024)(128)(2,1)}), bf16[153630]{0:T(1024)(128)(2,1)}) %all-reduce.20.cloned.1.call-update) | async-done | bytes 307276 | tf_op jit(solution)/shard_map/psum | solution.py:28
  (297 shorter events, 223.4 us)
Async XLA Ops:
  7.2 127.6 %all-gather.3.cloned.1.call-start = ((), (), s32[]{:S(2)}) async-start(), calls=%async_computation.1 | async-start | bytes 21565440 | tf_op jit(solution)/shard_map/all_gather | solution.py:18
  10.7 1221.5 %all-reduce.20.cloned.1.call-start = ((), (), s32[]{:S(2)}) async-start(), calls=%async_computation | async-start | bytes 618496 | tf_op jit(solution)/shard_map/psum | solution.py:28
  13.8 168.7 %copy-start.16 = (f32[512,64]{0,1:T(8,128)}, f32[512,64]{0,1:T(8,128)S(1)}, u32[]{:S(2)}) copy-start(f32[512,64]{0,1:T(8,128)S(1)} %get-tuple-element.266) | copy-start | bytes 393220
  13.8 168.7 %copy-start.18 = (f32[512,64]{0,1:T(8,128)}, f32[512,64]{0,1:T(8,128)S(1)}, u32[]{:S(2)}) copy-start(f32[512,64]{0,1:T(8,128)S(1)} %get-tuple-element.267) | copy-start | bytes 393220
  912.1 193.5 %collective-permute-start.9 = (bf16[16,320]{1,0:T(8,128)(2,1)S(1)}, bf16[16,320]{1,0:T(8,128)(2,1)S(1)}, u32[]{:S(2)}, u32[]{:S(2)}) collective-permute-start(bf16[16,320]{1,0:T(8,128)(2,1)S(1)} %convert.74), channel_id=1, source_target_pairs={{0,2},{1,3},{2,4},{3,5},{4,6},{5,7},{6,8},{7,9},{8,10},{9,11},{10,... | collective-permute-start | bytes 30728
  913.4 194.2 %collective-permute-start.10 = (bf16[16,320]{1,0:T(8,128)(2,1)S(1)}, bf16[16,320]{1,0:T(8,128)(2,1)S(1)}, u32[]{:S(2)}, u32[]{:S(2)}) collective-permute-start(bf16[16,320]{1,0:T(8,128)(2,1)S(1)} %convert.74), channel_id=1, source_target_pairs={{0,3},{1,4},{2,5},{3,6},{4,7},{5,8},{6,9},{7,10},{8,11},{9,12},{10... | collective-permute-start | bytes 30728
  921.4 187.5 %collective-permute-start.8 = (bf16[16,320]{1,0:T(8,128)(2,1)S(1)}, bf16[16,320]{1,0:T(8,128)(2,1)S(1)}, u32[]{:S(2)}, u32[]{:S(2)}) collective-permute-start(bf16[16,320]{1,0:T(8,128)(2,1)S(1)} %convert.74), channel_id=1, source_target_pairs={{0,1},{1,2},{2,3},{3,4},{4,5},{5,6},{6,7},{7,8},{8,9},{9,10},{10,1... | collective-permute-start | bytes 30728
  923.3 181.0 %collective-permute-start.11 = (bf16[15,320]{1,0:T(8,128)(2,1)S(1)}, bf16[15,320]{1,0:T(8,128)(2,1)S(1)}, u32[]{:S(2)}, u32[]{:S(2)}) collective-permute-start(bf16[15,320]{1,0:T(8,128)(2,1)S(1)} %slice.153), channel_id=1, source_target_pairs={{0,4},{1,5},{2,6},{3,7},{4,8},{5,9},{6,10},{7,11},{8,12},{9,13},{1... | collective-permute-start | bytes 28808
  1103.0 11.5 collective-permute-start.5
  1104.3 13.9 %collective-permute-start.6 = (bf16[16,320]{1,0:T(8,128)(2,1)S(1)}, bf16[16,320]{1,0:T(8,128)(2,1)S(1)}, u32[]{:S(2)}, u32[]{:S(2)}) collective-permute-start(bf16[16,320]{1,0:T(8,128)(2,1)S(1)} %convert.75), channel_id=1, source_target_pairs={{0,3},{1,4},{2,5},{3,6},{4,7},{5,8},{6,9},{7,10},{8,11},{9,12},{10... | collective-permute-start | bytes 30728
  1105.7 13.9 %collective-permute-start.4 = (bf16[16,320]{1,0:T(8,128)(2,1)S(1)}, bf16[16,320]{1,0:T(8,128)(2,1)S(1)}, u32[]{:S(2)}, u32[]{:S(2)}) collective-permute-start(bf16[16,320]{1,0:T(8,128)(2,1)S(1)} %convert.75), channel_id=1, source_target_pairs={{0,1},{1,2},{2,3},{3,4},{4,5},{5,6},{6,7},{7,8},{8,9},{9,10},{10,1... | collective-permute-start | bytes 30728
  1107.6 3.3 collective-permute-start.7
  1108.9 16.3 %collective-permute-start.1 = (bf16[16,960]{1,0:T(8,128)(2,1)S(1)}, bf16[16,960]{1,0:T(8,128)(2,1)S(1)}, u32[]{:S(2)}, u32[]{:S(2)}) collective-permute-start(bf16[16,960]{1,0:T(8,128)(2,1)S(1)} %convert.73), channel_id=1, source_target_pairs={{0,2},{1,3},{2,4},{3,5},{4,6},{5,7},{6,8},{7,9},{8,10},{9,11},{10,... | collective-permute-start | bytes 92168
  1110.9 18.2 %collective-permute-start.2 = (bf16[16,960]{1,0:T(8,128)(2,1)S(1)}, bf16[16,960]{1,0:T(8,128)(2,1)S(1)}, u32[]{:S(2)}, u32[]{:S(2)}) collective-permute-start(bf16[16,960]{1,0:T(8,128)(2,1)S(1)} %convert.73), channel_id=1, source_target_pairs={{0,3},{1,4},{2,5},{3,6},{4,7},{5,8},{6,9},{7,10},{8,11},{9,12},{10... | collective-permute-start | bytes 92168
  1114.6 15.8 %collective-permute-start = (bf16[16,960]{1,0:T(8,128)(2,1)S(1)}, bf16[16,960]{1,0:T(8,128)(2,1)S(1)}, u32[]{:S(2)}, u32[]{:S(2)}) collective-permute-start(bf16[16,960]{1,0:T(8,128)(2,1)S(1)} %convert.73), channel_id=1, source_target_pairs={{0,1},{1,2},{2,3},{3,4},{4,5},{5,6},{6,7},{7,8},{8,9},{9,10},{10,1... | collective-permute-start | bytes 92168
  1118.2 5.7 collective-permute-start.3
  1119.5 18.6 %collective-permute-start.21 = (bf16[960,16]{0,1:T(8,128)(2,1)S(1)}, bf16[960,16]{0,1:T(8,128)(2,1)S(1)}, u32[]{:S(2)}, u32[]{:S(2)}) collective-permute-start(bf16[960,16]{0,1:T(8,128)(2,1)S(1)} %convert.72), channel_id=1, source_target_pairs={{0,2},{1,3},{2,4},{3,5},{4,6},{5,7},{6,8},{7,9},{8,10},{9,11},{10,... | collective-permute-start | bytes 92168
  1123.9 18.6 %collective-permute-start.22 = (bf16[960,16]{0,1:T(8,128)(2,1)S(1)}, bf16[960,16]{0,1:T(8,128)(2,1)S(1)}, u32[]{:S(2)}, u32[]{:S(2)}) collective-permute-start(bf16[960,16]{0,1:T(8,128)(2,1)S(1)} %convert.72), channel_id=1, source_target_pairs={{0,3},{1,4},{2,5},{3,6},{4,7},{5,8},{6,9},{7,10},{8,11},{9,12},{10... | collective-permute-start | bytes 92168
  1125.2 20.7 %collective-permute-start.20 = (bf16[960,16]{0,1:T(8,128)(2,1)S(1)}, bf16[960,16]{0,1:T(8,128)(2,1)}, u32[]{:S(2)}, u32[]{:S(2)}) collective-permute-start(bf16[960,16]{0,1:T(8,128)(2,1)S(1)} %convert.72), channel_id=1, source_target_pairs={{0,1},{1,2},{2,3},{3,4},{4,5},{5,6},{6,7},{7,8},{8,9},{9,10},{10,1... | collective-permute-start | bytes 92168
  1129.1 6.5 collective-permute-start.23
  1130.4 23.1 %collective-permute-start.25 = (bf16[2560,16]{0,1:T(8,128)(2,1)S(1)}, bf16[2560,16]{0,1:T(8,128)(2,1)S(1)}, u32[]{:S(2)}, u32[]{:S(2)}) collective-permute-start(bf16[2560,16]{0,1:T(8,128)(2,1)S(1)} %convert.69), channel_id=1, source_target_pairs={{0,2},{1,3},{2,4},{3,5},{4,6},{5,7},{6,8},{7,9},{8,10},{9,11},{10,... | collective-permute-start | bytes 245768
  1135.6 22.9 %collective-permute-start.26 = (bf16[2560,16]{0,1:T(8,128)(2,1)S(1)}, bf16[2560,16]{0,1:T(8,128)(2,1)S(1)}, u32[]{:S(2)}, u32[]{:S(2)}) collective-permute-start(bf16[2560,16]{0,1:T(8,128)(2,1)S(1)} %convert.69), channel_id=1, source_target_pairs={{0,3},{1,4},{2,5},{3,6},{4,7},{5,8},{6,9},{7,10},{8,11},{9,12},{10... | collective-permute-start | bytes 245768
  1138.1 27.0 %collective-permute-start.24 = (bf16[2560,16]{0,1:T(8,128)(2,1)S(1)}, bf16[2560,16]{0,1:T(8,128)(2,1)S(1)}, u32[]{:S(2)}, u32[]{:S(2)}) collective-permute-start(bf16[2560,16]{0,1:T(8,128)(2,1)S(1)} %convert.69), channel_id=1, source_target_pairs={{0,1},{1,2},{2,3},{3,4},{4,5},{5,6},{6,7},{7,8},{8,9},{9,10},{10,1... | collective-permute-start | bytes 245768
  1142.5 9.2 collective-permute-start.27
  1145.9 24.0 %collective-permute-start.17 = (bf16[16,2560]{1,0:T(8,128)(2,1)}, bf16[16,2560]{1,0:T(8,128)(2,1)S(1)}, u32[]{:S(2)}, u32[]{:S(2)}) collective-permute-start(bf16[16,2560]{1,0:T(8,128)(2,1)} %convert.70), channel_id=1, source_target_pairs={{0,2},{1,3},{2,4},{3,5},{4,6},{5,7},{6,8},{7,9},{8,10},{9,11},{10,... | collective-permute-start | bytes 245768
  1151.7 24.0 %collective-permute-start.18 = (bf16[16,2560]{1,0:T(8,128)(2,1)}, bf16[16,2560]{1,0:T(8,128)(2,1)S(1)}, u32[]{:S(2)}, u32[]{:S(2)}) collective-permute-start(bf16[16,2560]{1,0:T(8,128)(2,1)} %convert.70), channel_id=1, source_target_pairs={{0,3},{1,4},{2,5},{3,6},{4,7},{5,8},{6,9},{7,10},{8,11},{9,12},{10... | collective-permute-start | bytes 245768
  1153.5 32.1 %collective-permute-start.16 = (bf16[16,2560]{1,0:T(8,128)(2,1)}, bf16[16,2560]{1,0:T(8,128)(2,1)}, u32[]{:S(2)}, u32[]{:S(2)}) collective-permute-start(bf16[16,2560]{1,0:T(8,128)(2,1)} %convert.70), channel_id=1, source_target_pairs={{0,1},{1,2},{2,3},{3,4},{4,5},{5,6},{6,7},{7,8},{8,9},{9,10},{10,1... | collective-permute-start | bytes 245768
  1158.5 9.5 collective-permute-start.19
  1165.2 23.1 %collective-permute-start.13 = (bf16[16,2560]{1,0:T(8,128)(2,1)}, bf16[16,2560]{1,0:T(8,128)(2,1)S(1)}, u32[]{:S(2)}, u32[]{:S(2)}) collective-permute-start(bf16[16,2560]{1,0:T(8,128)(2,1)} %convert.71), channel_id=1, source_target_pairs={{0,2},{1,3},{2,4},{3,5},{4,6},{5,7},{6,8},{7,9},{8,10},{9,11},{10,... | collective-permute-start | bytes 245768
  1168.0 20.3 %collective-permute-start.14 = (bf16[16,2560]{1,0:T(8,128)(2,1)}, bf16[16,2560]{1,0:T(8,128)(2,1)S(1)}, u32[]{:S(2)}, u32[]{:S(2)}) collective-permute-start(bf16[16,2560]{1,0:T(8,128)(2,1)} %convert.71), channel_id=1, source_target_pairs={{0,3},{1,4},{2,5},{3,6},{4,7},{5,8},{6,9},{7,10},{8,11},{9,12},{10... | collective-permute-start | bytes 245768
  1169.9 18.4 %collective-permute-start.12 = (bf16[16,2560]{1,0:T(8,128)(2,1)}, bf16[16,2560]{1,0:T(8,128)(2,1)S(1)}, u32[]{:S(2)}, u32[]{:S(2)}) collective-permute-start(bf16[16,2560]{1,0:T(8,128)(2,1)} %convert.71), channel_id=1, source_target_pairs={{0,1},{1,2},{2,3},{3,4},{4,5},{5,6},{6,7},{7,8},{8,9},{9,10},{10,1... | collective-permute-start | bytes 245768
  1175.7 12.6 %collective-permute-start.15 = (bf16[15,2560]{1,0:T(8,128)(2,1)}, bf16[15,2560]{1,0:T(8,128)(2,1)S(1)}, u32[]{:S(2)}, u32[]{:S(2)}) collective-permute-start(bf16[15,2560]{1,0:T(8,128)(2,1)} %slice.154), channel_id=1, source_target_pairs={{0,4},{1,5},{2,6},{3,7},{4,8},{5,9},{6,10},{7,11},{8,12},{9,13},{1... | collective-permute-start | bytes 230408
  (55 other events, 846.9 us)
Sparse Core Ops, SparseCore 0:
  11.7 123.1 all-gather.2
  1199.2 33.0 all-reduce.19
where the time goes:
time: 1260 us; the launch traced here: 1250 us
  blocking collectives  629 us (50%)
  matrix products  215 us (17%)
  waiting for transfers between devices  145 us (12%)
  local copies, waits for them, and re-layouts  106 us (8%)
  starting transfers between devices  90.1 us (7%)
  other arithmetic  47.5 us (4%)
  between operations  17.1 us (1%)
    unnamed x2, blocking collectives  629 us
    all_gather x1, waiting for transfers between devices, gather_turned(): lax.all_gather(both, axis, axis=0, tiled=True)  118 us
    unnamed x28, starting transfers between devices  90 us
    dot_general x7, matrix products, contract_product(): lax.dot_general(left, weight, (((1,), (1,)), ((), ())), preferred_element...  52.3 us
    unnamed x102, local copies, waits for them, and re-layouts  38.9 us
    dot_general x7, matrix products, tdot(): lax.dot_general(left, right, (((0,), (0,)), ((), ())), preferred_element_...  36.5 us
    psum x1, waiting for transfers between devices, packed_total(): so_far = lax.psum(vector, axis)  27 us
  transfers between devices with their start and end apart: 30, of which 2 were waited for; matrix products, arithmetic and copies ran while one was open for 2% of the time, Pallas kernels for 0%

commit v1 on v0

--- a/solution.py
+++ b/solution.py
@@ -12,10 +12,17 @@
 EPSILON = 1e-05
 
 
+def _create_gates(m, shard_axis):
+    current_arr = lax.psum(1, shard_axis)
+    arr_next = jnp.stack([m] * current_arr, 0)
+    t1 = lax.all_to_all(arr_next, shard_axis, 0, 0)
+    return jnp.concatenate(t1, 0)
+
+
 def gather_turned(arrays, axis, dims):
     turned = [jnp.moveaxis(a, dim, 0) for a, dim in zip(arrays, dims)]
     both = jnp.concatenate([t.reshape(len(t), -1) for t in turned], axis=1)
-    whole, at, finished = (lax.all_gather(both, axis, axis=0, tiled=True), 0, [])
+    whole, at, finished = (_create_gates(both, shard_axis=axis), 0, [])
     for t, dim in zip(turned, dims):
         section = whole[:, at : at + t[0].size].reshape(-1, *t.shape[1:])
         finished.append(jnp.moveaxis(section, 0, dim))

time: 1260 us -> 1480 us (1.17)
  waiting for transfers between devices: 145 us -> 328 us
  blocking collectives: 629 us -> 651 us
    all_to_all x0 -> x1, waiting for transfers between devices: none -> 301 us  [_create_gates(): t1 = lax.all_to_all(arr_next, shard_axis, 0, 0)]
    all_gather x1 -> x0, waiting for transfers between devices: 118 us -> none  [gather_turned(): lax.all_gather(both, axis, axis=0, tiled=True)]
    unnamed x2, blocking collectives: 629 us -> 651 us
    unnamed x102 -> x103, local copies, waits for them, and re-layouts: 38.9 us -> 18.1 us
    reshape x0 -> x1, local copies, waits for them, and re-layouts: none -> 20.1 us  [_create_gates(): return jnp.concatenate(t1, 0)]
where the time goes in v1:
time: 1480 us; the launch traced here: 1470 us
  blocking collectives  651 us (44%)
  waiting for transfers between devices  328 us (22%)
  matrix products  215 us (15%)
  local copies, waits for them, and re-layouts  112 us (8%)
  starting transfers between devices  98.5 us (7%)
  other arithmetic  45.8 us (3%)
  between operations  17.1 us (1%)
    unnamed x2, blocking collectives  651 us
    all_to_all x1, waiting for transfers between devices, _create_gates(): t1 = lax.all_to_all(arr_next, shard_axis, 0, 0)  301 us
    unnamed x28, starting transfers between devices  85.8 us
    dot_general x7, matrix products, contract_product(): lax.dot_general(left, weight, (((1,), (1,)), ((), ())), preferred_element...  52.3 us
    dot_general x7, matrix products, tdot(): lax.dot_general(left, right, (((0,), (0,)), ((), ())), preferred_element_...  36.5 us
  transfers between devices with their start and end apart: 30, of which 2 were waited for; matrix products, arithmetic and copies ran while one was open for 2% of the time, Pallas kernels for 0%

profile of v1, /device:TPU:1, one launch (start us, length us, event | category | flops | bytes accessed | tf_op | source)
XLA Modules:
  0.0 1468.0 jit_solution(24826479735629516)
XLA Ops:
  9.9 7.3 stack.2
  17.2 12.6 all-to-all-start
  33.3 300.8 %all-to-all-done = bf16[64,15,10242]{2,1,0:T(8,128)(2,1)} async-done(((bf16[64,15,10242]{2,1,0:T(8,128)(2,1)}), bf16[64,15,10242]{2,1,0:T(8,128)(2,1)}, u32[]{:S(2)}, u32[]{:S(2)}) %all-to-all-start) | async-done | bytes 19664672 | tf_op jit(solution)/shard_map/all_to_all | solution.py:18
  334.1 20.1 %reshape.286 = bf16[960,10242]{1,0:T(8,128)(2,1)} reshape(bf16[64,15,10242]{2,1,0:T(8,128)(2,1)} %all-to-all-done) | data formatting | bytes 39329280 | tf_op jit(solution)/shard_map/reshape | solution.py:19
  371.5 6.4 reshape.289
  384.1 50.4 %while.26 = (s32[]{:T(128)}, bf16[2,512,5,3,64]{1,4,3,2,0:T(8,128)(2,1)}, f32[2,5,3,512]{3,2,1,0:T(4,128)}, bf16[2,512,5,64]{1,3,2,0:T(8,128)(2,1)S(1)}, bf16[2,...) while((s32[]{:T(128)}, bf16[2,512,5,3,64]{1,4,3,2,0:T(8,128)(2,1)}, ...), condition=%wide.region_4.5_spmd, body=%wide.region_1.4_spmd.sunk | while | flops 1050632704 | bytes 67375304 | solution.py:161
  384.2 6.9 fusion.180
  391.2 8.9 exponential_reduce_fusion.2
  400.1 7.8 fusion.181
  409.3 6.9 fusion.180
  416.2 8.9 exponential_reduce_fusion.2
  425.1 7.8 fusion.181
  445.8 11.7 fusion.78
  457.6 10.7 fusion.68
  468.2 19.1 %fusion.65 = (bf16[1024,2560]{1,0:T(8,128)(2,1)}, bf16[1024,2560]{1,0:T(8,128)(2,1)}, bf16[1024,2560]{1,0:T(8,128)(2,1)}) fusion(f32[2560,1024]{0,1:T(8,128)} %fusion.68, f32[1024,2560]{1,0:T(8,128)} %fusion.78, bf16[1024,960]{0,1:T(8,128)(2,1)} %copy-done.23, bf16[960,10242]{1,0:T(8,128)(2,1)} %reshape.286), kind=kOutput, calls=%fused_computation.68 | convolution fusion | flops 5075107840 | bytes 43581440 | tf_op jit(solution)/shard_map/dot_general | solution.py:167
  487.4 9.1 fusion.72
  496.5 9.1 multiply_reduce_fusion
  517.2 6.2 reshape.291
  526.7 59.5 %while.27 = (s32[]{:T(128)}, f32[2,512,5,3,64]{1,4,3,2,0:T(8,128)}, f32[2,512,5,64]{1,3,2,0:T(8,128)}, bf16[2,512,5,64]{1,3,2,0:T(8,128)(2,1)}, bf16[2,512,5,64]...) while((s32[]{:T(128)}, f32[2,512,5,3,64]{1,4,3,2,0:T(8,128)}, ...), condition=%wide.region_9.10_spmd, body=%wide.region_7.9_spmd.sunk | while | flops 2558779904 | bytes 186770704 | solution.py:280
  541.9 8.6 fusion.194
  571.5 8.6 fusion.194
  612.0 8.0 fusion.136
  620.0 7.7 fusion.137
  627.7 9.0 add_convert_fusion
  636.7 7.8 fusion.138
  647.6 476.8 %fusion.127 = (f32[16,960]{1,0:T(8,128)S(1)}, f32[16,320]{1,0:T(8,128)S(1)}, f32[16,320]{1,0:T(8,128)S(1)}, f32[16,2560]{1,0:T(8,128)S(1)}, f32[16,2560]{1,0:T(8...) fusion(f32[960,960]{1,0:T(8,128)} %fusion.122, f32[960,320]{1,0:T(8,128)} %fusion.120, ...), kind=kCustom, calls=%all-reduce-scatter.7 | all-reduce-scatter fusion | flops 10485761 | bytes 39977472
  1132.1 7.2 fusion.87
  1142.6 173.9 %all-reduce.16 = (bf16[960]{0:T(1024)(128)(2,1)S(1)}, bf16[960]{0:T(1024)(128)(2,1)S(1)}) all-reduce(f32[960]{0:T(1024)S(1)} %get-tuple-element.177, f32[960]{0:T(1024)S(1)} %copy-done.38), channel_id=9, replica_groups=mesh['replica'=2,'shard'=64] {'shard'}, use_global_device_ids=true, to_apply=%region_19.20.clone | all-reduce | flops 1920 | bytes 11520
  1391.6 11.1 collective-permute-start.15
  1407.8 8.3 concatenate.45
  1416.2 6.2 fusion.84
  1422.4 27.2 %all-reduce.20.cloned.1.call-done = bf16[153630]{0:T(1024)(128)(2,1)} async-done(((bf16[153630]{0:T(1024)(128)(2,1)}), bf16[153630]{0:T(1024)(128)(2,1)}) %all-reduce.20.cloned.1.call-update) | async-done | bytes 307276 | tf_op jit(solution)/shard_map/psum | solution.py:35
  (299 shorter events, 229.5 us)
Async XLA Ops:
  17.2 316.9 %all-to-all-start = ((bf16[64,15,10242]{2,1,0:T(8,128)(2,1)}), bf16[64,15,10242]{2,1,0:T(8,128)(2,1)}, u32[]{:S(2)}, u32[]{:S(2)}) async-start(bf16[64,15,10242]{2,1,0:T(8,128)(2,1)} %stack.2), calls=%async_computation | async-start | bytes 42467328 | tf_op jit(solution)/shard_map/all_to_all | solution.py:18
  29.8 1419.7 %all-reduce.20.cloned.1.call-start = ((), (), s32[]{:S(2)}) async-start(), calls=%async_computation.1 | async-start | bytes 618496 | tf_op jit(solution)/shard_map/psum | solution.py:35
  32.2 349.6 %copy-start.16 = (f32[512,64]{0,1:T(8,128)}, f32[512,64]{0,1:T(8,128)S(1)}, u32[]{:S(2)}) copy-start(f32[512,64]{0,1:T(8,128)S(1)} %get-tuple-element.266) | copy-start | bytes 393220
  32.2 349.5 %copy-start.18 = (f32[512,64]{0,1:T(8,128)}, f32[512,64]{0,1:T(8,128)S(1)}, u32[]{:S(2)}) copy-start(f32[512,64]{0,1:T(8,128)S(1)} %get-tuple-element.267) | copy-start | bytes 393220
  1124.5 195.8 %collective-permute-start.9 = (bf16[16,320]{1,0:T(8,128)(2,1)S(1)}, bf16[16,320]{1,0:T(8,128)(2,1)S(1)}, u32[]{:S(2)}, u32[]{:S(2)}) collective-permute-start(bf16[16,320]{1,0:T(8,128)(2,1)S(1)} %convert.74), channel_id=1, source_target_pairs={{0,2},{1,3},{2,4},{3,5},{4,6},{5,7},{6,8},{7,9},{8,10},{9,11},{10,... | collective-permute-start | bytes 30728
  1125.8 196.4 %collective-permute-start.10 = (bf16[16,320]{1,0:T(8,128)(2,1)S(1)}, bf16[16,320]{1,0:T(8,128)(2,1)S(1)}, u32[]{:S(2)}, u32[]{:S(2)}) collective-permute-start(bf16[16,320]{1,0:T(8,128)(2,1)S(1)} %convert.74), channel_id=1, source_target_pairs={{0,3},{1,4},{2,5},{3,6},{4,7},{5,8},{6,9},{7,10},{8,11},{9,12},{10... | collective-permute-start | bytes 30728
  1128.5 195.0 %collective-permute-start.8 = (bf16[16,320]{1,0:T(8,128)(2,1)S(1)}, bf16[16,320]{1,0:T(8,128)(2,1)S(1)}, u32[]{:S(2)}, u32[]{:S(2)}) collective-permute-start(bf16[16,320]{1,0:T(8,128)(2,1)S(1)} %convert.74), channel_id=1, source_target_pairs={{0,1},{1,2},{2,3},{3,4},{4,5},{5,6},{6,7},{7,8},{8,9},{9,10},{10,1... | collective-permute-start | bytes 30728
  1130.4 188.5 %collective-permute-start.11 = (bf16[15,320]{1,0:T(8,128)(2,1)S(1)}, bf16[15,320]{1,0:T(8,128)(2,1)S(1)}, u32[]{:S(2)}, u32[]{:S(2)}) collective-permute-start(bf16[15,320]{1,0:T(8,128)(2,1)S(1)} %slice.153), channel_id=1, source_target_pairs={{0,4},{1,5},{2,6},{3,7},{4,8},{5,9},{6,10},{7,11},{8,12},{9,13},{1... | collective-permute-start | bytes 28808
  1317.6 13.6 collective-permute-start.5
  1318.9 14.3 collective-permute-start.6
  1320.2 14.3 collective-permute-start.4
  1322.2 3.3 collective-permute-start.7
  1323.5 18.4 %collective-permute-start.1 = (bf16[16,960]{1,0:T(8,128)(2,1)S(1)}, bf16[16,960]{1,0:T(8,128)(2,1)S(1)}, u32[]{:S(2)}, u32[]{:S(2)}) collective-permute-start(bf16[16,960]{1,0:T(8,128)(2,1)S(1)} %convert.73), channel_id=1, source_target_pairs={{0,2},{1,3},{2,4},{3,5},{4,6},{5,7},{6,8},{7,9},{8,10},{9,11},{10,... | collective-permute-start | bytes 92168
  1325.5 20.3 %collective-permute-start.2 = (bf16[16,960]{1,0:T(8,128)(2,1)S(1)}, bf16[16,960]{1,0:T(8,128)(2,1)S(1)}, u32[]{:S(2)}, u32[]{:S(2)}) collective-permute-start(bf16[16,960]{1,0:T(8,128)(2,1)S(1)} %convert.73), channel_id=1, source_target_pairs={{0,3},{1,4},{2,5},{3,6},{4,7},{5,8},{6,9},{7,10},{8,11},{9,12},{10... | collective-permute-start | bytes 92168
  1331.3 15.8 %collective-permute-start = (bf16[16,960]{1,0:T(8,128)(2,1)S(1)}, bf16[16,960]{1,0:T(8,128)(2,1)S(1)}, u32[]{:S(2)}, u32[]{:S(2)}) collective-permute-start(bf16[16,960]{1,0:T(8,128)(2,1)S(1)} %convert.73), channel_id=1, source_target_pairs={{0,1},{1,2},{2,3},{3,4},{4,5},{5,6},{6,7},{7,8},{8,9},{9,10},{10,1... | collective-permute-start | bytes 92168
  1333.2 7.4 collective-permute-start.3
  1334.5 20.5 %collective-permute-start.21 = (bf16[960,16]{0,1:T(8,128)(2,1)S(1)}, bf16[960,16]{0,1:T(8,128)(2,1)S(1)}, u32[]{:S(2)}, u32[]{:S(2)}) collective-permute-start(bf16[960,16]{0,1:T(8,128)(2,1)S(1)} %convert.72), channel_id=1, source_target_pairs={{0,2},{1,3},{2,4},{3,5},{4,6},{5,7},{6,8},{7,9},{8,10},{9,11},{10,... | collective-permute-start | bytes 92168
  1340.6 18.8 %collective-permute-start.22 = (bf16[960,16]{0,1:T(8,128)(2,1)S(1)}, bf16[960,16]{0,1:T(8,128)(2,1)S(1)}, u32[]{:S(2)}, u32[]{:S(2)}) collective-permute-start(bf16[960,16]{0,1:T(8,128)(2,1)S(1)} %convert.72), channel_id=1, source_target_pairs={{0,3},{1,4},{2,5},{3,6},{4,7},{5,8},{6,9},{7,10},{8,11},{9,12},{10... | collective-permute-start | bytes 92168
  1341.9 20.9 %collective-permute-start.20 = (bf16[960,16]{0,1:T(8,128)(2,1)S(1)}, bf16[960,16]{0,1:T(8,128)(2,1)}, u32[]{:S(2)}, u32[]{:S(2)}) collective-permute-start(bf16[960,16]{0,1:T(8,128)(2,1)S(1)} %convert.72), channel_id=1, source_target_pairs={{0,1},{1,2},{2,3},{3,4},{4,5},{5,6},{6,7},{7,8},{8,9},{9,10},{10,1... | collective-permute-start | bytes 92168
  1345.8 6.7 collective-permute-start.23
  1347.1 23.3 %collective-permute-start.25 = (bf16[2560,16]{0,1:T(8,128)(2,1)S(1)}, bf16[2560,16]{0,1:T(8,128)(2,1)S(1)}, u32[]{:S(2)}, u32[]{:S(2)}) collective-permute-start(bf16[2560,16]{0,1:T(8,128)(2,1)S(1)} %convert.69), channel_id=1, source_target_pairs={{0,2},{1,3},{2,4},{3,5},{4,6},{5,7},{6,8},{7,9},{8,10},{9,11},{10,... | collective-permute-start | bytes 245768
  1352.5 22.9 %collective-permute-start.26 = (bf16[2560,16]{0,1:T(8,128)(2,1)S(1)}, bf16[2560,16]{0,1:T(8,128)(2,1)S(1)}, u32[]{:S(2)}, u32[]{:S(2)}) collective-permute-start(bf16[2560,16]{0,1:T(8,128)(2,1)S(1)} %convert.69), channel_id=1, source_target_pairs={{0,3},{1,4},{2,5},{3,6},{4,7},{5,8},{6,9},{7,10},{8,11},{9,12},{10... | collective-permute-start | bytes 245768
  1355.0 26.1 %collective-permute-start.24 = (bf16[2560,16]{0,1:T(8,128)(2,1)S(1)}, bf16[2560,16]{0,1:T(8,128)(2,1)S(1)}, u32[]{:S(2)}, u32[]{:S(2)}) collective-permute-start(bf16[2560,16]{0,1:T(8,128)(2,1)S(1)} %convert.69), channel_id=1, source_target_pairs={{0,1},{1,2},{2,3},{3,4},{4,5},{5,6},{6,7},{7,8},{8,9},{9,10},{10,1... | collective-permute-start | bytes 245768
  1359.4 9.2 collective-permute-start.27
  1362.7 23.1 %collective-permute-start.17 = (bf16[16,2560]{1,0:T(8,128)(2,1)}, bf16[16,2560]{1,0:T(8,128)(2,1)S(1)}, u32[]{:S(2)}, u32[]{:S(2)}) collective-permute-start(bf16[16,2560]{1,0:T(8,128)(2,1)} %convert.70), channel_id=1, source_target_pairs={{0,2},{1,3},{2,4},{3,5},{4,6},{5,7},{6,8},{7,9},{8,10},{9,11},{10,... | collective-permute-start | bytes 245768
  1368.6 23.0 %collective-permute-start.18 = (bf16[16,2560]{1,0:T(8,128)(2,1)}, bf16[16,2560]{1,0:T(8,128)(2,1)S(1)}, u32[]{:S(2)}, u32[]{:S(2)}) collective-permute-start(bf16[16,2560]{1,0:T(8,128)(2,1)} %convert.70), channel_id=1, source_target_pairs={{0,3},{1,4},{2,5},{3,6},{4,7},{5,8},{6,9},{7,10},{8,11},{9,12},{10... | collective-permute-start | bytes 245768
  1370.4 32.3 %collective-permute-start.16 = (bf16[16,2560]{1,0:T(8,128)(2,1)}, bf16[16,2560]{1,0:T(8,128)(2,1)}, u32[]{:S(2)}, u32[]{:S(2)}) collective-permute-start(bf16[16,2560]{1,0:T(8,128)(2,1)} %convert.70), channel_id=1, source_target_pairs={{0,1},{1,2},{2,3},{3,4},{4,5},{5,6},{6,7},{7,8},{8,9},{9,10},{10,1... | collective-permute-start | bytes 245768
  1375.4 8.6 collective-permute-start.19
  1381.1 24.3 %collective-permute-start.13 = (bf16[16,2560]{1,0:T(8,128)(2,1)}, bf16[16,2560]{1,0:T(8,128)(2,1)S(1)}, u32[]{:S(2)}, u32[]{:S(2)}) collective-permute-start(bf16[16,2560]{1,0:T(8,128)(2,1)} %convert.71), channel_id=1, source_target_pairs={{0,2},{1,3},{2,4},{3,5},{4,6},{5,7},{6,8},{7,9},{8,10},{9,11},{10,... | collective-permute-start | bytes 245768
  1384.0 21.5 %collective-permute-start.14 = (bf16[16,2560]{1,0:T(8,128)(2,1)}, bf16[16,2560]{1,0:T(8,128)(2,1)S(1)}, u32[]{:S(2)}, u32[]{:S(2)}) collective-permute-start(bf16[16,2560]{1,0:T(8,128)(2,1)} %convert.71), channel_id=1, source_target_pairs={{0,3},{1,4},{2,5},{3,6},{4,7},{5,8},{6,9},{7,10},{8,11},{9,12},{10... | collective-permute-start | bytes 245768
  1385.8 19.6 %collective-permute-start.12 = (bf16[16,2560]{1,0:T(8,128)(2,1)}, bf16[16,2560]{1,0:T(8,128)(2,1)S(1)}, u32[]{:S(2)}, u32[]{:S(2)}) collective-permute-start(bf16[16,2560]{1,0:T(8,128)(2,1)} %convert.71), channel_id=1, source_target_pairs={{0,1},{1,2},{2,3},{3,4},{4,5},{5,6},{6,7},{7,8},{8,9},{9,10},{10,1... | collective-permute-start | bytes 245768
  1391.6 13.8 collective-permute-start.15
  (56 other events, 911.3 us)
Sparse Core Ops, SparseCore 0:
  1416.3 33.1 all-reduce.19
